TPU v7x, 32 devices: a whole 2x2x4 slice. The times are simulated.
32 devices in a mesh: wide: 4 (over x, core), narrow: 8 (over z, y).
Axes of the slice: x: 2, y: 2, z: 4, core: 2. Of those that a mesh axis runs over, the one named last changes fastest.
Arguments:
- photo_embeds: bfloat16 [8192, 1152], P(('wide', 'narrow')), may hold values from -2.5 to 2.5
- caption_vectors: bfloat16 [8192, 1152], P(('wide', 'narrow')), may hold values from -2.5 to 2.5
- positive_match_index: int32 [8192], P(('wide', 'narrow')), may hold values from 0 to 1023
- trained_logscale_param: float32 [1], replicated, may hold values from 2 to 8
- offset_bias_array: float32 [1], replicated, may hold values from -4 to -1
Outputs:
- grad_images: float32 [8192, 1152], P(('wide', 'narrow'))
- grad_texts: float32 [8192, 1152], P(('wide', 'narrow'))
Inputs may be any that keep to these rules, and one draw needn't show every extreme that they name: `positive_match_index`: labels of an image name one of the 1024 texts that its block meets, s * 256 + j for column j of the block met at step s.
All inputs are finite; a program needn't handle non-finite values.
Results may differ from a plain program's by a relative error of at most 0.0022.
Values may be sent and summed in bfloat16 or wider, within the bound.
A program may use at most 64 MiB of HBM per device.

v0:
```python
import functools

import jax
import jax.numpy as jnp
from jax import lax
from jax.experimental import pallas as pl
from jax.experimental.pallas import tpu as pltpu
from jax.sharding import PartitionSpec as P

STEPS = 4
CHUNKS = 4
AHEAD = 2
LAG_Z = 3
LAG_Y = 0
MESH = pl.DeviceIdType.MESH


def slope_tile(left, right, labels, text_axis, first, scale, shift):
    score = scale * lax.dot_general(
        left, right, (((1,), (1,)), ((), ())), preferred_element_type=jnp.float32
    ) + shift
    match = labels == lax.broadcasted_iota(jnp.int32, score.shape, text_axis) + first
    half = jax.nn.sigmoid(jnp.where(match, -score, score))
    return jnp.where(match, -half, half).astype(jnp.bfloat16)


def kernel(
    wide,
    narrow,
    scale_ref,
    shift_ref,
    label_hbm,
    image_hbm,
    text_hbm,
    grad_image_ref,
    grad_text_ref,
    label_ref,
    image_ref,
    text_ref,
    texts,
    images,
    labels,
    label_column,
    loaded,
    text_arrival,
    image_arrival,
    label_arrival,
    departure,
    label_departure,
):
    devices = wide * narrow
    me = lax.axis_index("wide") * narrow + lax.axis_index("narrow")
    odd = lax.rem(me, 2)
    rows = image_ref.shape[0]
    part = rows // CHUNKS

    def place(by):
        at = lax.rem(me + by + devices, devices)
        return (lax.div(at, narrow), lax.rem(at, narrow))

    barrier = pltpu.get_barrier_semaphore()
    near = [by for s in range(1, STEPS) for by in (s, -s)]
    for by in near:
        pl.semaphore_signal(barrier, inc=1, device_id=place(by), device_id_type=MESH)
    loads = [
        pltpu.make_async_copy(src, dst, loaded.at[at])
        for at, (src, dst) in enumerate(
            (
                (image_hbm, image_ref),
                (text_hbm, text_ref),
                (label_hbm, label_ref),
            )
        )
    ]
    for load in loads:
        load.start()
    for load in loads:
        load.wait()
    pl.semaphore_wait(barrier, len(near))

    def label_copy(s):
        return pltpu.make_async_remote_copy(
            src_ref=label_ref,
            dst_ref=labels.at[s - 1],
            send_sem=label_departure.at[s - 1],
            recv_sem=label_arrival.at[s - 1],
            device_id=place(-s),
            device_id_type=MESH,
        )

    def routes(own_major, major, major_arrival, own_minor, minor, minor_arrival, d):
        def send(lane, src, dst, arrival, slot, by):
            def chunk(c):
                span = pl.ds(c * part, part)
                return pltpu.make_async_remote_copy(
                    src_ref=src.at[span],
                    dst_ref=dst.at[slot].at[span],
                    send_sem=departure.at[lane, c],
                    recv_sem=arrival.at[slot, c],
                    device_id=place(by),
                    device_id_type=MESH,
                )

            return chunk

        return (
            send(0, own_minor, minor, minor_arrival, 1, -2 * d),
            send(1, own_major, major, major_arrival, 1, 2 * d),
            send(2, own_major, major, major_arrival, 0, d),
            send(3, minor.at[1], minor, minor_arrival, 0, d),
            send(4, major.at[1], major, major_arrival, 2, d),
            send(5, major.at[0], major, major_arrival, 2, 2 * d),
        )

    text_side = (text_ref, texts, text_arrival)
    image_side = (image_ref, images, image_arrival)

    def both(body):
        @pl.when(odd == 0)
        def _():
            body(routes(*text_side, *image_side, 1), text_side, image_side)

        @pl.when(odd == 1)
        def _():
            body(routes(*image_side, *text_side, -1), image_side, text_side)

    def landed(side, slot, c):
        _, buffer, arrival = side
        here = buffer.at[slot].at[pl.ds(c * part, part)]
        pltpu.make_async_copy(here, here, arrival.at[slot, c]).wait()

    def begin(lanes, major, minor):
        for c in range(CHUNKS):
            lanes[0](c).start()
            lanes[1](c).start()
            if c < AHEAD:
                lanes[2](c).start()

    both(begin)
    for s in range(1, STEPS):
        label_copy(s).start()

    scale, shift = scale_ref[0], shift_ref[0]
    label_column[...] = jnp.broadcast_to(label_ref[...], (rows, rows)).T

    def image_share(s, at=0, size=rows):
        span = pl.ds(at, size)
        block = text_ref[span] if s == 0 else texts[s - 1, span]
        slope = slope_tile(
            image_ref[...], block, label_column[:, :size], 1, s * rows + at, scale, shift
        )
        return jnp.dot(slope, block, preferred_element_type=jnp.float32)

    def text_share(s, at=0, size=rows):
        span = pl.ds(at, size)
        block = image_ref[span] if s == 0 else images[s - 1, span]
        own = label_ref[:, span] if s == 0 else labels[s - 1, :, span]
        slope = slope_tile(text_ref[...], block, own, 0, s * rows, scale, shift)
        return jnp.dot(slope, block, preferred_element_type=jnp.float32)

    def relay(start, stop):
        def body(lanes, major, minor):
            for t in range(start, stop):
                if t < CHUNKS:
                    landed(minor, 1, t)
                    lanes[3](t).start()
                    if t + AHEAD < CHUNKS:
                        lanes[2](t + AHEAD).start()
                if 0 <= t - LAG_Z < CHUNKS:
                    landed(major, 0, t - LAG_Z)
                    lanes[5](t - LAG_Z).start()
                if 0 <= t - LAG_Y < CHUNKS:
                    landed(major, 1, t - LAG_Y)
                    lanes[4](t - LAG_Y).start()

        return body

    end = CHUNKS + max(LAG_Z, LAG_Y)
    both(relay(0, 2))
    grad_image_ref[...] = image_share(0)
    both(relay(2, 4))
    grad_text_ref[...] = text_share(0)
    both(relay(4, end))

    def rest(lanes, major, minor):
        for c in range(CHUNKS):
            landed(minor, 0, c)

    for s in range(1, STEPS):
        label_copy(s).wait_recv()
    grad_image_ref[...] += image_share(2)
    grad_text_ref[...] += text_share(2)
    both(rest)
    grad_image_ref[...] += image_share(1)
    grad_text_ref[...] += text_share(1)

    def add_text(s):
        grad_text_ref[...] += text_share(s)

    def add_image(s):
        grad_image_ref[...] += image_share(s)

    def last(lanes, major, minor):
        first, second = (add_text, add_image) if major is text_side else (add_image, add_text)
        for c in range(CHUNKS):
            landed(minor, 2, c)
        first(STEPS - 1)
        for c in range(CHUNKS):
            landed(major, 2, c)
        second(STEPS - 1)

    both(last)

    def finish(lanes, major, minor):
        for lane in lanes:
            for c in range(CHUNKS):
                lane(c).wait_send()

    both(finish)
    for s in range(1, STEPS):
        label_copy(s).wait_send()


def on_device(wide, narrow, photo, caption, match_index, logscale, offset):
    rows, width = photo.shape
    here = pl.BlockSpec(memory_space=pltpu.HBM)
    smem = pl.BlockSpec(memory_space=pltpu.SMEM)
    vmem = pl.BlockSpec(memory_space=pltpu.VMEM)
    operands = [
        pltpu.with_memory_space_constraint(array, pltpu.HBM)
        for array in (match_index.reshape(1, rows), photo, caption)
    ]
    out = pltpu.VMEM((rows, width), jnp.float32)
    tiles = 4 * STEPS * rows * rows * width
    grad_photo, grad_caption = pl.pallas_call(
        functools.partial(kernel, wide, narrow),
        out_shape=(out, out),
        in_specs=[smem] * 2 + [here] * 3,
        out_specs=(vmem, vmem),
        scratch_shapes=[
            pltpu.VMEM((1, rows), jnp.int32),
            pltpu.VMEM((rows, width), jnp.bfloat16),
            pltpu.VMEM((rows, width), jnp.bfloat16),
            pltpu.VMEM((STEPS - 1, rows, width), jnp.bfloat16),
            pltpu.VMEM((STEPS - 1, rows, width), jnp.bfloat16),
            pltpu.VMEM((STEPS - 1, 1, rows), jnp.int32),
            pltpu.VMEM((rows, rows), jnp.int32),
            pltpu.SemaphoreType.DMA((3,)),
            pltpu.SemaphoreType.DMA((STEPS - 1, CHUNKS)),
            pltpu.SemaphoreType.DMA((STEPS - 1, CHUNKS)),
            pltpu.SemaphoreType.DMA((STEPS - 1,)),
            pltpu.SemaphoreType.DMA((6, CHUNKS)),
            pltpu.SemaphoreType.DMA((STEPS - 1,)),
        ],
        compiler_params=pltpu.CompilerParams(
            collective_id=0, has_side_effects=True, vmem_limit_bytes=32 * 1024 * 1024
        ),
        cost_estimate=pl.CostEstimate(
            flops=2 * tiles, bytes_accessed=6 * rows * width * 2, transcendentals=0
        ),
        name="sigmoid_ring",
    )(logscale, offset, *operands)
    return logscale[0] * grad_photo, logscale[0] * grad_caption


def solution(mesh):
    pairs = ("wide", "narrow")
    return jax.shard_map(
        functools.partial(on_device, mesh.shape["wide"], mesh.shape["narrow"]),
        mesh=mesh,
        in_specs=(P(pairs, None), P(pairs, None), P(pairs), P(), P()),
        out_specs=(P(pairs, None), P(pairs, None)),
        check_vma=False,
    )
```

profile of v0, /device:TPU:0, one launch (start us, length us, event | category | flops | bytes accessed | tf_op | source)
XLA Modules:
  0.0 51.8 jit_solution(6133246628886476386)
XLA Ops:
  1.9 48.4 %sigmoid_ring.1 = (f32[256,1152]{1,0:T(8,128)S(1)}, f32[256,1152]{1,0:T(8,128)S(1)}) custom-call(f32[1]{0:T(128)} %copy.7.scale_ref, f32[1]{0:T(128)S(6)} %copy.8.shift_ref, s32[1,256]{1,0:T(1,128)} %bitcast.3, bf16[256,1152]{1,0:T(8,128)(2,1)} %image_hbm.1, bf16[256,1152]{1,0:T(8,128)(2,1)} %text_hbm.1), custom_call_target="tpu_custom_call" | custom-call | flops 2415919104 | bytes 3538944 | tf_op jit(solution)/shard_map/sigmoid_ring/pallas_call | solution.py:235
  50.3 1.6 %broadcast_multiply_fusion = (f32[256,1152]{1,0:T(8,128)}, f32[256,1152]{1,0:T(8,128)}) fusion(f32[256,1152]{1,0:T(8,128)S(1)} %get-tuple-element.5, f32[]{:T(128)} %bitcast.2, f32[256,1152]{1,0:T(8,128)S(1)} %get-tuple-element.4), kind=kLoop, calls=%fused_computation | loop fusion | flops 589824 | bytes 4718596 | tf_op jit(solution)/shard_map/mul | solution.py:263
where the time goes:
time: 52 us; the launch traced here: 51.8 us
  Pallas kernels  48.4 us (93%)
  between operations  1.93 us (4%)
  other arithmetic  1.56 us (3%)
    pallas_call x1, Pallas kernels, on_device(): pl.pallas_call(functools.partial(kernel, wide, narrow), out_shape=(out, o...  48.4 us
    mul x1, other arithmetic, on_device(): return (logscale[0] * grad_photo, logscale[0] * grad_caption)  1.56 us

commit v1 on v0

--- a/solution.py
+++ b/solution.py
@@ -12,6 +12,7 @@
 AHEAD = 2
 LAG_Z = 3
 LAG_Y = 0
+PIECES = 2
 MESH = pl.DeviceIdType.MESH
 
 
@@ -34,13 +35,13 @@
     text_hbm,
     grad_image_ref,
     grad_text_ref,
-    label_ref,
     image_ref,
     text_ref,
     texts,
     images,
     labels,
     label_column,
+    label_ref,
     loaded,
     text_arrival,
     image_arrival,
@@ -149,14 +150,14 @@
         slope = slope_tile(
             image_ref[...], block, label_column[:, :size], 1, s * rows + at, scale, shift
         )
-        return jnp.dot(slope, block, preferred_element_type=jnp.float32)
+        return scale * jnp.dot(slope, block, preferred_element_type=jnp.float32)
 
     def text_share(s, at=0, size=rows):
         span = pl.ds(at, size)
         block = image_ref[span] if s == 0 else images[s - 1, span]
         own = label_ref[:, span] if s == 0 else labels[s - 1, :, span]
         slope = slope_tile(text_ref[...], block, own, 0, s * rows, scale, shift)
-        return jnp.dot(slope, block, preferred_element_type=jnp.float32)
+        return scale * jnp.dot(slope, block, preferred_element_type=jnp.float32)
 
     def relay(start, stop):
         def body(lanes, major, minor):
@@ -175,39 +176,39 @@
 
         return body
 
+    def add_text(s):
+        grad_text_ref[...] += text_share(s)
+
+    def add_image(s):
+        grad_image_ref[...] += image_share(s)
+
     end = CHUNKS + max(LAG_Z, LAG_Y)
     both(relay(0, 2))
     grad_image_ref[...] = image_share(0)
     both(relay(2, 4))
     grad_text_ref[...] = text_share(0)
-    both(relay(4, end))
+    both(relay(4, 5))
+    for s in range(1, STEPS):
+        label_copy(s).wait_recv()
+    add_image(2)
+    both(relay(5, 6))
+    add_text(2)
+    both(relay(6, end))
 
     def rest(lanes, major, minor):
         for c in range(CHUNKS):
             landed(minor, 0, c)
 
-    for s in range(1, STEPS):
-        label_copy(s).wait_recv()
-    grad_image_ref[...] += image_share(2)
-    grad_text_ref[...] += text_share(2)
     both(rest)
-    grad_image_ref[...] += image_share(1)
-    grad_text_ref[...] += text_share(1)
-
-    def add_text(s):
-        grad_text_ref[...] += text_share(s)
-
-    def add_image(s):
-        grad_image_ref[...] += image_share(s)
+    add_image(1)
+    add_text(1)
 
     def last(lanes, major, minor):
-        first, second = (add_text, add_image) if major is text_side else (add_image, add_text)
         for c in range(CHUNKS):
             landed(minor, 2, c)
-        first(STEPS - 1)
+        (add_text if major is text_side else add_image)(STEPS - 1)
         for c in range(CHUNKS):
             landed(major, 2, c)
-        second(STEPS - 1)
 
     both(last)
 
@@ -219,6 +220,59 @@
     both(finish)
     for s in range(1, STEPS):
         label_copy(s).wait_send()
+
+
+def tail_kernel(
+    narrow,
+    scale_ref,
+    shift_ref,
+    grad_image_ref,
+    grad_text_ref,
+    image_ref,
+    text_ref,
+    texts,
+    images,
+    labels,
+    label_column,
+    image_out,
+    text_out,
+    stage,
+    stored,
+):
+    odd = lax.rem(lax.axis_index("wide") * narrow + lax.axis_index("narrow"), 2)
+    scale, shift = scale_ref[0], shift_ref[0]
+    rows = image_ref.shape[0]
+    size, s = rows // PIECES, STEPS - 1
+
+    def close(done, done_out, part_ref, out, own_ref, block_ref, slope_of):
+        stores = [pltpu.make_async_copy(done, done_out, stored.at[PIECES])]
+        stores[0].start()
+        block = block_ref[s - 1]
+        for piece in range(PIECES):
+            span = pl.ds(piece * size, size)
+            slope = slope_of(own_ref[span], block, piece * size, span)
+            stage[span] = part_ref[span] + scale * jnp.dot(
+                slope, block, preferred_element_type=jnp.float32
+            )
+            store = pltpu.make_async_copy(stage.at[span], out.at[span], stored.at[piece])
+            store.start()
+            stores.append(store)
+        for store in stores:
+            store.wait()
+
+    @pl.when(odd == 0)
+    def _():
+        def slope_of(own, block, at, span):
+            return slope_tile(own, block, label_column[span], 1, s * rows, scale, shift)
+
+        close(grad_text_ref, text_out, grad_image_ref, image_out, image_ref, texts, slope_of)
+
+    @pl.when(odd == 1)
+    def _():
+        def slope_of(own, block, at, span):
+            return slope_tile(own, block, labels[s - 1], 0, s * rows + at, scale, shift)
+
+        close(grad_image_ref, image_out, grad_text_ref, text_out, text_ref, images, slope_of)
 
 
 def on_device(wide, narrow, photo, caption, match_index, logscale, offset):
@@ -230,21 +284,24 @@
         pltpu.with_memory_space_constraint(array, pltpu.HBM)
         for array in (match_index.reshape(1, rows), photo, caption)
     ]
-    out = pltpu.VMEM((rows, width), jnp.float32)
+    held = (
+        pltpu.VMEM((rows, width), jnp.float32),
+        pltpu.VMEM((rows, width), jnp.float32),
+        pltpu.VMEM((rows, width), jnp.bfloat16),
+        pltpu.VMEM((rows, width), jnp.bfloat16),
+        pltpu.VMEM((STEPS - 1, rows, width), jnp.bfloat16),
+        pltpu.VMEM((STEPS - 1, rows, width), jnp.bfloat16),
+        pltpu.VMEM((STEPS - 1, 1, rows), jnp.int32),
+        pltpu.VMEM((rows, rows), jnp.int32),
+    )
     tiles = 4 * STEPS * rows * rows * width
-    grad_photo, grad_caption = pl.pallas_call(
+    results = pl.pallas_call(
         functools.partial(kernel, wide, narrow),
-        out_shape=(out, out),
+        out_shape=held,
         in_specs=[smem] * 2 + [here] * 3,
-        out_specs=(vmem, vmem),
+        out_specs=(vmem,) * len(held),
         scratch_shapes=[
             pltpu.VMEM((1, rows), jnp.int32),
-            pltpu.VMEM((rows, width), jnp.bfloat16),
-            pltpu.VMEM((rows, width), jnp.bfloat16),
-            pltpu.VMEM((STEPS - 1, rows, width), jnp.bfloat16),
-            pltpu.VMEM((STEPS - 1, rows, width), jnp.bfloat16),
-            pltpu.VMEM((STEPS - 1, 1, rows), jnp.int32),
-            pltpu.VMEM((rows, rows), jnp.int32),
             pltpu.SemaphoreType.DMA((3,)),
             pltpu.SemaphoreType.DMA((STEPS - 1, CHUNKS)),
             pltpu.SemaphoreType.DMA((STEPS - 1, CHUNKS)),
@@ -260,7 +317,19 @@
         ),
         name="sigmoid_ring",
     )(logscale, offset, *operands)
-    return logscale[0] * grad_photo, logscale[0] * grad_caption
+    out = jax.ShapeDtypeStruct((rows, width), jnp.float32)
+    return pl.pallas_call(
+        functools.partial(tail_kernel, narrow),
+        out_shape=(out, out),
+        in_specs=[smem] * 2 + [vmem] * len(held),
+        out_specs=(here, here),
+        scratch_shapes=[
+            pltpu.VMEM((rows, width), jnp.float32),
+            pltpu.SemaphoreType.DMA((PIECES + 1,)),
+        ],
+        compiler_params=pltpu.CompilerParams(vmem_limit_bytes=16 * 1024 * 1024),
+        name="sigmoid_tail",
+    )(logscale, offset, *results)
 
 
 def solution(mesh):

time: 52 us -> 51.6 us (level)
  other arithmetic: 1.56 us -> 0 us
  Pallas kernels: 48.4 us -> 49.5 us
    mul x1 -> x0, other arithmetic: 1.56 us -> none  [on_device(): return (logscale[0] * grad_photo, logscale[0] * grad_caption)]
    pallas_call x1 -> x2, Pallas kernels: 48.4 us -> 49.5 us  [the longest x1 47.3 us: on_device(): pl.pallas_call(functools.partial(kernel, wide, narrow), out_shape=held, i...]
where the time goes in v1:
time: 51.6 us; the launch traced here: 51.4 us
  Pallas kernels  49.5 us (96%)
  between operations  1.93 us (4%)
    pallas_call x1, Pallas kernels, on_device(): pl.pallas_call(functools.partial(kernel, wide, narrow), out_shape=held, i...  47.3 us
    pallas_call x1, Pallas kernels, on_device(): pl.pallas_call(functools.partial(tail_kernel, narrow), out_shape=(out, ou...  2.18 us

profile of v1, /device:TPU:0, one launch (start us, length us, event | category | flops | bytes accessed | tf_op | source)
XLA Modules:
  0.0 51.4 jit_solution(9692888500027677119)
XLA Ops:
  1.9 47.3 %sigmoid_ring.1 = (f32[256,1152]{1,0:T(8,128)S(1)}, f32[256,1152]{1,0:T(8,128)S(1)}, bf16[256,1152]{1,0:T(8,128)(2,1)S(1)}, bf16[256,1152]{1,0:T(8,128)(2,1)S(1)...) custom-call(f32[1]{0:T(128)S(6)} %copy.7.scale_ref, ...), custom_call_target="tpu_custom_call" | custom-call | flops 2415919104 | bytes 3538944 | tf_op jit(solution)/shard_map/sigmoid_ring/pallas_call | solution.py:298
  49.2 2.2 %sigmoid_tail.1 = (f32[256,1152]{1,0:T(8,128)}, f32[256,1152]{1,0:T(8,128)}) custom-call(f32[1]{0:T(128)S(6)} %copy.7.scale_ref, f32[1]{0:T(128)S(6)} %copy.8.shift_ref, f32[256,1152]{1,0:T(8,128)S(1)} %get-tuple-element.10.grad_image_ref, f32[256,1152]{1,0:T(8,128)S(1)} %get-tuple-element.11.grad_text_ref, ...), custom_call_target="tpu_custom_call" | custom-call | tf_op jit(solution)/shard_map/sigmoid_tail/pallas_call | solution.py:321

commit v2 on v1

--- a/solution.py
+++ b/solution.py
@@ -10,9 +10,8 @@
 STEPS = 4
 CHUNKS = 4
 AHEAD = 2
-LAG_Z = 3
-LAG_Y = 0
-PIECES = 2
+PIECES = 1
+HEAD = 0
 MESH = pl.DeviceIdType.MESH
 
 
@@ -59,10 +58,19 @@
         at = lax.rem(me + by + devices, devices)
         return (lax.div(at, narrow), lax.rem(at, narrow))
 
-    barrier = pltpu.get_barrier_semaphore()
-    near = [by for s in range(1, STEPS) for by in (s, -s)]
-    for by in near:
-        pl.semaphore_signal(barrier, inc=1, device_id=place(by), device_id_type=MESH)
+    column, row = lax.axis_index("wide"), lax.axis_index("narrow")
+    low, top = row < 2, row >= narrow - 2
+
+    def across(by):
+        return (lax.rem(column + by + wide, wide), row)
+
+    def tell(semaphore, device):
+        pl.semaphore_signal(semaphore, inc=1, device_id=device, device_id_type=MESH)
+
+    def either(test, yes, no):
+        pl.when(test)(yes)
+        pl.when(jnp.logical_not(test))(no)
+
     loads = [
         pltpu.make_async_copy(src, dst, loaded.at[at])
         for at, (src, dst) in enumerate(
@@ -73,30 +81,24 @@
             )
         )
     ]
+    barrier = pltpu.get_barrier_semaphore()
+    tell(barrier, place(1 - 2 * odd))
+    tell(barrier, place(2))
+    tell(barrier, place(-2))
     for load in loads:
         load.start()
+    pl.semaphore_wait(barrier, 3)
     for load in loads:
         load.wait()
-    pl.semaphore_wait(barrier, len(near))
-
-    def label_copy(s):
-        return pltpu.make_async_remote_copy(
-            src_ref=label_ref,
-            dst_ref=labels.at[s - 1],
-            send_sem=label_departure.at[s - 1],
-            recv_sem=label_arrival.at[s - 1],
-            device_id=place(-s),
-            device_id_type=MESH,
-        )
 
     def routes(own_major, major, major_arrival, own_minor, minor, minor_arrival, d):
         def send(lane, src, dst, arrival, slot, by):
-            def chunk(c):
-                span = pl.ds(c * part, part)
+            def chunk(c, size=part):
+                span = pl.ds(c * part, size)
                 return pltpu.make_async_remote_copy(
                     src_ref=src.at[span],
                     dst_ref=dst.at[slot].at[span],
-                    send_sem=departure.at[lane, c],
+                    send_sem=departure.at[lane],
                     recv_sem=arrival.at[slot, c],
                     device_id=place(by),
                     device_id_type=MESH,
@@ -130,16 +132,72 @@
         here = buffer.at[slot].at[pl.ds(c * part, part)]
         pltpu.make_async_copy(here, here, arrival.at[slot, c]).wait()
 
+    def label_lane(lane, src, slot, by):
+        return pltpu.make_async_remote_copy(
+            src_ref=src,
+            dst_ref=labels.at[slot],
+            send_sem=label_departure.at[lane],
+            recv_sem=label_arrival.at[slot],
+            device_id=place(by),
+            device_id_type=MESH,
+        )
+
+    own_label = label_lane(0, label_ref, 1, -2)
+    even_label = (label_lane(1, labels.at[1], 0, 1),)
+    odd_label = (
+        label_lane(1, label_ref, 0, -1),
+        label_lane(2, labels.at[1], 2, -1),
+        label_lane(3, labels.at[0], 2, -2),
+    )
+
+    def label_landed(slot):
+        here = labels.at[slot]
+        pltpu.make_async_copy(here, here, label_arrival.at[slot]).wait()
+
+    def near_far(lanes, major):
+        ahead, behind = (lanes[1], lanes[0]) if major is text_side else lanes[:2]
+        return ahead, behind
+
     def begin(lanes, major, minor):
+        ahead, behind = near_far(lanes, major)
+        inner = jnp.logical_not(jnp.logical_or(low, top))
+        pl.when(jnp.logical_not(low))(own_label.start)
         for c in range(CHUNKS):
-            lanes[0](c).start()
-            lanes[1](c).start()
+            if c < HEAD:
+                pl.when(jnp.logical_not(low))(behind(c).start)
+                pl.when(jnp.logical_not(top))(ahead(c).start)
+            else:
+
+                @pl.when(inner)
+                def _():
+                    behind(c).start()
+                    ahead(c).start()
+
             if c < AHEAD:
                 lanes[2](c).start()
+        if major is image_side:
+            odd_label[0].start()
+
+    def wrap(lanes, major, minor):
+        ahead, behind = near_far(lanes, major)
+
+        def mixed(far, near):
+            for c in range(CHUNKS):
+                far(c).start()
+                if c + HEAD < CHUNKS:
+                    near(c + HEAD).start()
+
+        @pl.when(low)
+        def _():
+            own_label.start()
+            mixed(behind, ahead)
+
+        @pl.when(top)
+        def _():
+            mixed(ahead, behind)
 
     both(begin)
-    for s in range(1, STEPS):
-        label_copy(s).start()
+    both(wrap)
 
     scale, shift = scale_ref[0], shift_ref[0]
     label_column[...] = jnp.broadcast_to(label_ref[...], (rows, rows)).T
@@ -159,22 +217,23 @@
         slope = slope_tile(text_ref[...], block, own, 0, s * rows, scale, shift)
         return scale * jnp.dot(slope, block, preferred_element_type=jnp.float32)
 
-    def relay(start, stop):
+    def relay(*steps):
         def body(lanes, major, minor):
-            for t in range(start, stop):
-                if t < CHUNKS:
-                    landed(minor, 1, t)
-                    lanes[3](t).start()
-                    if t + AHEAD < CHUNKS:
-                        lanes[2](t + AHEAD).start()
-                if 0 <= t - LAG_Z < CHUNKS:
-                    landed(major, 0, t - LAG_Z)
-                    lanes[5](t - LAG_Z).start()
-                if 0 <= t - LAG_Y < CHUNKS:
-                    landed(major, 1, t - LAG_Y)
-                    lanes[4](t - LAG_Y).start()
-
-        return body
+            source = {3: (minor, 1), 4: (major, 1), 5: (major, 0)}
+            if major is text_side:
+                tags = {(3, 0): (1, even_label[0])}
+            else:
+                tags = {(4, 0): (1, odd_label[1]), (5, 0): (0, odd_label[2])}
+            for lane, c in steps:
+                if (lane, c) in tags:
+                    slot, copy = tags[lane, c]
+                    label_landed(slot)
+                    copy.start()
+                if lane in source:
+                    landed(*source[lane], c)
+                lanes[lane](c).start()
+
+        both(body)
 
     def add_text(s):
         grad_text_ref[...] += text_share(s)
@@ -182,23 +241,20 @@
     def add_image(s):
         grad_image_ref[...] += image_share(s)
 
-    end = CHUNKS + max(LAG_Z, LAG_Y)
-    both(relay(0, 2))
+    relay((3, 0), (2, 2))
     grad_image_ref[...] = image_share(0)
-    both(relay(2, 4))
+    relay((3, 1), (2, 3))
     grad_text_ref[...] = text_share(0)
-    both(relay(4, 5))
-    for s in range(1, STEPS):
-        label_copy(s).wait_recv()
+    relay((4, 0), (3, 2), (4, 1), (3, 3), (4, 2), (5, 0), (4, 3), (5, 1), (5, 2), (5, 3))
     add_image(2)
-    both(relay(5, 6))
     add_text(2)
-    both(relay(6, end))
 
     def rest(lanes, major, minor):
         for c in range(CHUNKS):
             landed(minor, 0, c)
 
+    pl.when(odd == 0)(lambda: label_landed(0))
+    label_landed(2)
     both(rest)
     add_image(1)
     add_text(1)
@@ -214,12 +270,12 @@
 
     def finish(lanes, major, minor):
         for lane in lanes:
-            for c in range(CHUNKS):
-                lane(c).wait_send()
+            lane(0, rows).wait_send()
+        own_label.wait_send()
+        for lane in even_label if major is text_side else odd_label:
+            lane.wait_send()
 
     both(finish)
-    for s in range(1, STEPS):
-        label_copy(s).wait_send()
 
 
 def tail_kernel(
@@ -306,8 +362,8 @@
             pltpu.SemaphoreType.DMA((STEPS - 1, CHUNKS)),
             pltpu.SemaphoreType.DMA((STEPS - 1, CHUNKS)),
             pltpu.SemaphoreType.DMA((STEPS - 1,)),
-            pltpu.SemaphoreType.DMA((6, CHUNKS)),
-            pltpu.SemaphoreType.DMA((STEPS - 1,)),
+            pltpu.SemaphoreType.DMA((6,)),
+            pltpu.SemaphoreType.DMA((4,)),
         ],
         compiler_params=pltpu.CompilerParams(
             collective_id=0, has_side_effects=True, vmem_limit_bytes=32 * 1024 * 1024

time: 51.6 us -> 51 us (0.988)
  Pallas kernels: 49.5 us -> 48.9 us
where the time goes in v2:
time: 51 us; the launch traced here: 50.8 us
  Pallas kernels  48.9 us (96%)
  between operations  1.93 us (4%)
    pallas_call x1, Pallas kernels, on_device(): pl.pallas_call(functools.partial(kernel, wide, narrow), out_shape=held, i...  46.9 us
    pallas_call x1, Pallas kernels, on_device(): pl.pallas_call(functools.partial(tail_kernel, narrow), out_shape=(out, ou...  1.99 us

profile of v2, /device:TPU:0, one launch (start us, length us, event | category | flops | bytes accessed | tf_op | source)
XLA Modules:
  0.0 50.8 jit_solution(1038870184808146530)
XLA Ops:
  1.9 46.9 %sigmoid_ring.1 = (f32[256,1152]{1,0:T(8,128)S(1)}, f32[256,1152]{1,0:T(8,128)S(1)}, bf16[256,1152]{1,0:T(8,128)(2,1)S(1)}, bf16[256,1152]{1,0:T(8,128)(2,1)S(1)...) custom-call(f32[1]{0:T(128)S(6)} %copy.7.scale_ref, ...), custom_call_target="tpu_custom_call" | custom-call | flops 2415919104 | bytes 3538944 | tf_op jit(solution)/shard_map/sigmoid_ring/pallas_call | solution.py:354
  48.8 2.0 %sigmoid_tail.1 = (f32[256,1152]{1,0:T(8,128)}, f32[256,1152]{1,0:T(8,128)}) custom-call(f32[1]{0:T(128)S(6)} %copy.7.scale_ref, f32[1]{0:T(128)S(6)} %copy.8.shift_ref, f32[256,1152]{1,0:T(8,128)S(1)} %get-tuple-element.10.grad_image_ref, f32[256,1152]{1,0:T(8,128)S(1)} %get-tuple-element.11.grad_text_ref, ...), custom_call_target="tpu_custom_call" | custom-call | tf_op jit(solution)/shard_map/sigmoid_tail/pallas_call | solution.py:377

commit v3 on v2

--- a/solution.py
+++ b/solution.py
@@ -10,7 +10,7 @@
 STEPS = 4
 CHUNKS = 4
 AHEAD = 2
-PIECES = 1
+PIECES = 4
 HEAD = 0
 MESH = pl.DeviceIdType.MESH
 
@@ -297,20 +297,21 @@
 ):
     odd = lax.rem(lax.axis_index("wide") * narrow + lax.axis_index("narrow"), 2)
     scale, shift = scale_ref[0], shift_ref[0]
-    rows = image_ref.shape[0]
-    size, s = rows // PIECES, STEPS - 1
+    rows, width = image_ref.shape
+    s = STEPS - 1
+    cuts = [width * piece // PIECES // 256 * 256 for piece in range(PIECES)] + [width]
 
     def close(done, done_out, part_ref, out, own_ref, block_ref, slope_of):
         stores = [pltpu.make_async_copy(done, done_out, stored.at[PIECES])]
         stores[0].start()
-        block = block_ref[s - 1]
+        block = block_ref.at[s - 1]
+        slope = slope_of(own_ref[...], block[...])
         for piece in range(PIECES):
-            span = pl.ds(piece * size, size)
-            slope = slope_of(own_ref[span], block, piece * size, span)
-            stage[span] = part_ref[span] + scale * jnp.dot(
-                slope, block, preferred_element_type=jnp.float32
+            at = pl.ds(cuts[piece], cuts[piece + 1] - cuts[piece])
+            stage[:, at] = part_ref[:, at] + scale * jnp.dot(
+                slope, block[:, at], preferred_element_type=jnp.float32
             )
-            store = pltpu.make_async_copy(stage.at[span], out.at[span], stored.at[piece])
+            store = pltpu.make_async_copy(stage.at[:, at], out.at[:, at], stored.at[piece])
             store.start()
             stores.append(store)
         for store in stores:
@@ -318,15 +319,15 @@
 
     @pl.when(odd == 0)
     def _():
-        def slope_of(own, block, at, span):
-            return slope_tile(own, block, label_column[span], 1, s * rows, scale, shift)
+        def slope_of(own, block):
+            return slope_tile(own, block, label_column[...], 1, s * rows, scale, shift)
 
         close(grad_text_ref, text_out, grad_image_ref, image_out, image_ref, texts, slope_of)
 
     @pl.when(odd == 1)
     def _():
-        def slope_of(own, block, at, span):
-            return slope_tile(own, block, labels[s - 1], 0, s * rows + at, scale, shift)
+        def slope_of(own, block):
+            return slope_tile(own, block, labels[s - 1], 0, s * rows, scale, shift)
 
         close(grad_image_ref, image_out, grad_text_ref, text_out, text_ref, images, slope_of)
 

time: 51 us -> 50.8 us (level)
  no operation moved by 1% of the time
where the time goes in v3:
time: 50.8 us; the launch traced here: 50.6 us
  Pallas kernels  48.6 us (96%)
  between operations  1.93 us (4%)
    pallas_call x1, Pallas kernels, on_device(): pl.pallas_call(functools.partial(kernel, wide, narrow), out_shape=held, i...  46.9 us
    pallas_call x1, Pallas kernels, on_device(): pl.pallas_call(functools.partial(tail_kernel, narrow), out_shape=(out, ou...  1.75 us

profile of v3, /device:TPU:0, one launch (start us, length us, event | category | flops | bytes accessed | tf_op | source)
XLA Modules:
  0.0 50.6 jit_solution(9916171694384047445)
XLA Ops:
  1.9 46.9 %sigmoid_ring.1 = (f32[256,1152]{1,0:T(8,128)S(1)}, f32[256,1152]{1,0:T(8,128)S(1)}, bf16[256,1152]{1,0:T(8,128)(2,1)S(1)}, bf16[256,1152]{1,0:T(8,128)(2,1)S(1)...) custom-call(f32[1]{0:T(128)S(6)} %copy.7.scale_ref, ...), custom_call_target="tpu_custom_call" | custom-call | flops 2415919104 | bytes 3538944 | tf_op jit(solution)/shard_map/sigmoid_ring/pallas_call | solution.py:355
  48.8 1.7 %sigmoid_tail.1 = (f32[256,1152]{1,0:T(8,128)}, f32[256,1152]{1,0:T(8,128)}) custom-call(f32[1]{0:T(128)S(6)} %copy.7.scale_ref, f32[1]{0:T(128)S(6)} %copy.8.shift_ref, f32[256,1152]{1,0:T(8,128)S(1)} %get-tuple-element.10.grad_image_ref, f32[256,1152]{1,0:T(8,128)S(1)} %get-tuple-element.11.grad_text_ref, ...), custom_call_target="tpu_custom_call" | custom-call | tf_op jit(solution)/shard_map/sigmoid_tail/pallas_call | solution.py:378
